TPU v7x, 512 devices: a whole 4x4x16 slice. The times are simulated.
512 devices in a mesh: tok: 32 (over z, core), feat: 16 (over y, x).
Axes of the slice: x: 4, y: 4, z: 16, core: 2. Of those that a mesh axis runs over, the one named last changes fastest.
Arguments:
- tokens: bfloat16 [12288, 1408], P(('tok', 'feat')), may hold values from -24 to 24
- segment_ids: int32 [12288], P('tok'), may hold values from 0 to 1023, as said below
- owners: int32 [1024], P('tok'), may hold values from 0 to 31, as said below
- project_in: bfloat16 [1408, 3, 1408], P(None, None, 'feat'), may hold values from -2 to 2
- project_out: bfloat16 [1408, 1408], P('feat'), may hold values from -0.15625 to 0.15625
- weight_up: bfloat16 [1408, 6144], P('tok', 'feat'), may hold values from -0.15625 to 0.15625
- weight_down: bfloat16 [6144, 1408], P('feat', 'tok'), may hold values from -0.078125 to 0.078125
- weight_merge: bfloat16 [5632, 4096], P(None, 'feat'), may hold values from -0.078125 to 0.078125
- gain_attend: bfloat16 [1408], replicated, may hold values from 0.25 to 1.75
- gain_hidden: bfloat16 [1408], replicated, may hold values from 0.25 to 1.75
- gain_final: bfloat16 [1408], replicated, may hold values from 0.25 to 1.75
Outputs:
- routed: bfloat16 [16384, 4096], P('tok', 'feat')
Inputs may be any that keep to these rules, and one draw needn't show every extreme that they name: `segment_ids`: patches 384 * s to 384 * s + 383 form shard s; their ids never fall, run without gaps and lie in 32 * s to 32 * s + 31; in every shard but the last they start at 32 * s, in the last they end at 1023. Every segment has 16 to 64 patches, a multiple of 4, and every shard holds one of 64 patches. Each 2x2 window of an image is four consecutive patches. owners[g] is the tok index that owns segment g; the 32 entries from 32 * s to 32 * s + 31 are distinct.
All inputs are finite; a program needn't handle non-finite values.
Results may differ from a plain program's by a relative error of at most 0.025.
Values may be sent and summed in bfloat16 or wider, within the bound.
A program may use at most 64 MiB of HBM per device.

v0:
```python
import jax
import jax.numpy as jnp
from jax import lax
from jax.sharding import PartitionSpec as P

LEAST_UNITS = 4
MOST_UNITS = 16
HEAD_DIM = 88
epsilon = 1e-06


def layer_norm(row_block, gain_row):
    as_float = row_block.astype(jnp.float32)
    center = jnp.mean(as_float, axis=-1, keepdims=True)
    spread = jnp.mean(jnp.square(as_float - center), axis=-1, keepdims=True)
    scaled = (as_float - center) * lax.rsqrt(spread + epsilon) * gain_row.astype(jnp.float32)
    return scaled.astype(jnp.bfloat16)


def project_rows(row_block, weight_block):
    return jnp.dot(
        lax.all_gather(row_block, "feat", axis=0, tiled=True),
        weight_block,
        preferred_element_type=jnp.float32,
    )


def scatter_rows(left_rows, right_rows):
    return lax.psum_scatter(
        jnp.dot(left_rows, right_rows, preferred_element_type=jnp.float32).astype(jnp.bfloat16),
        "feat",
        scatter_dimension=0,
        tiled=True,
    ).astype(jnp.float32)


def early_weights(weight_up, weight_down):
    return (weight_up, weight_down)


def upper_weight(fetched):
    return lax.all_gather(fetched[0], "tok", axis=0, tiled=True)


def lower_weight(fetched):
    return lax.all_gather(fetched[1], "tok", axis=1, tiled=True)


def attend(projected, segment_ids, head_count):
    token_count = projected.shape[0]
    parts_all = projected.reshape(token_count, 3, head_count, HEAD_DIM)
    queries = (parts_all[:, 0] * HEAD_DIM ** (-0.5)).astype(jnp.bfloat16)
    keys_here = parts_all[:, 1].astype(jnp.bfloat16)
    values_here = parts_all[:, 2].astype(jnp.bfloat16)
    scores = jnp.einsum("qhd,khd->hqk", queries, keys_here, preferred_element_type=jnp.float32)
    same_segment = segment_ids[:, None] == segment_ids[None, :]
    scores = jnp.where(same_segment[None, :, :], scores, -1e30)
    highest = jnp.max(scores, axis=-1, keepdims=True)
    raised = jnp.exp(scores - highest)
    weights_soft = (raised / jnp.sum(raised, axis=-1, keepdims=True)).astype(jnp.bfloat16)
    attended = jnp.einsum(
        "hqk,khd->qhd", weights_soft, values_here, preferred_element_type=jnp.float32
    )
    return attended.astype(jnp.bfloat16).reshape(token_count, head_count * HEAD_DIM)


def route_rows(embedded, segment_ids, owners):
    merged_count = embedded.shape[0]
    peer_count = owners.shape[0]
    least_units = max(LEAST_UNITS, (merged_count + peer_count - 1) // peer_count)
    slot_count = max(MOST_UNITS, 2 * least_units)
    first_ids = segment_ids.reshape(merged_count, 4)[:, 0]
    id_base = lax.axis_index("tok") * peer_count
    local_index = first_ids - id_base
    owner_pick = local_index[:, None] == jnp.arange(peer_count, dtype=jnp.int32)[None, :]
    owner_of = jnp.sum(jnp.where(owner_pick, owners[None, :], 0), axis=1)
    row_index = jnp.arange(merged_count, dtype=jnp.int32)
    earlier = (row_index[None, :] < row_index[:, None]) & (first_ids[None, :] == first_ids[:, None])
    within = jnp.sum(earlier.astype(jnp.int32), axis=1)
    target = owner_of * slot_count + within
    select = (
        jnp.arange(peer_count * slot_count, dtype=jnp.int32)[:, None] == target[None, :]
    ).astype(jnp.bfloat16)
    packed = jnp.dot(select, embedded, preferred_element_type=jnp.float32).astype(jnp.bfloat16)
    packed = packed.reshape(peer_count, slot_count, embedded.shape[1])
    received = lax.all_to_all(packed, "tok", split_axis=0, concat_axis=0, tiled=True)
    return received.reshape(peer_count * slot_count, embedded.shape[1])


def body(
    tokens,
    segment_ids,
    owners,
    project_in,
    project_out,
    weight_up,
    weight_down,
    weight_merge,
    gain_attend,
    gain_hidden,
    gain_final,
):
    model_width = tokens.shape[1]
    head_count = project_in.shape[2] // HEAD_DIM
    fetched = early_weights(weight_up, weight_down)
    flat_in = project_in.reshape(model_width, 3 * project_in.shape[2])
    local_count = tokens.shape[0]
    normed = layer_norm(tokens, gain_attend)
    projected = project_rows(normed, flat_in)
    attended = attend(projected, segment_ids, head_count)
    second = (tokens.astype(jnp.float32) + scatter_rows(attended, project_out)).astype(jnp.bfloat16)
    normed_hidden = layer_norm(second, gain_hidden)
    hidden = jax.nn.gelu(
        project_rows(normed_hidden, upper_weight(fetched)), approximate=False
    ).astype(jnp.bfloat16)
    residual_out = (
        second.astype(jnp.float32) + scatter_rows(hidden, lower_weight(fetched))
    ).astype(jnp.bfloat16)
    normed_final = layer_norm(residual_out, gain_final)
    merged = normed_final.reshape(local_count // 4, 4 * model_width)
    embedded = project_rows(merged, weight_merge).astype(jnp.bfloat16)
    return route_rows(embedded, segment_ids, owners)


def solution(mesh):
    return jax.shard_map(
        body,
        mesh=mesh,
        in_specs=(
            P(("tok", "feat"), None),
            P("tok"),
            P("tok"),
            P(None, None, "feat"),
            P("feat", None),
            P("tok", "feat"),
            P("feat", "tok"),
            P(None, "feat"),
            P(),
            P(),
            P(),
        ),
        out_specs=P("tok", "feat"),
        check_vma=False,
    )
```

profile of v0, /device:TPU:1, one launch (start us, length us, event | category | flops | bytes accessed | tf_op | source)
XLA Modules:
  0.0 485.8 jit_solution(15327780551669928933)
XLA Ops:
  7.4 1.2 convert_reduce_fusion.1
  8.5 1.1 fusion.58
  9.6 0.7 convert_element_type.98
  10.3 1.6 fusion.60
  11.9 0.0 all-gather.9.cloned.1.call-update
  12.0 0.0 reduce-scatter.7.cloned.1.call-start
  12.0 62.1 %all-gather.9.cloned.1.call-done = bf16[384,1408]{1,0:T(8,128)(2,1)} async-done(((bf16[24,1408]{1,0:T(8,128)(2,1)}), bf16[384,1408]{1,0:T(8,128)(2,1)}) %all-gather.9.cloned.1.call-update) | async-done | bytes 1081360 | tf_op jit(solution)/shard_map/all_gather | solution.py:22
  74.1 2.0 fusion.104
  76.2 0.3 fusion.105
  76.5 0.4 copy-done.2
  76.8 0.1 fusion.13
  76.9 2.6 convolution_convert_fusion.1
  79.6 0.0 reduce-scatter.7.cloned.1.call-update
  79.6 0.0 all-gather.13.cloned.1.call-start
  79.7 0.5 all-gather.13.cloned.1.call-update
  80.2 0.0 all-gather.15.cloned.1.call-start
  80.2 0.5 all-gather.15.cloned.1.call-update
  80.8 0.0 all-gather.11.cloned.1.call-start
  80.8 86.1 %reduce-scatter.7.cloned.1.call-done = bf16[24,1408]{1,0:T(8,128)(2,1)} async-done(((bf16[384,1408]{1,0:T(8,128)(2,1)}), bf16[24,1408]{1,0:T(8,128)(2,1)}) %reduce-scatter.7.cloned.1.call-update) | async-done | bytes 67600
  167.0 1.0 convert_reduce_fusion
  168.0 0.2 fusion.55
  168.2 0.7 fusion.57
  168.9 0.0 all-gather.11.cloned.1.call-update
  169.0 0.0 reduce-scatter.9.cloned.1.call-start
  169.0 0.0 all-gather.13.cloned.1.call-done
  169.0 2.2 reshape.121
  171.2 53.8 %all-gather.15.cloned.1.call-done = bf16[32,44,384]{2,1,0:T(8,128)(2,1)} async-done(((bf16[1,44,384]{2,1,0:T(8,128)(2,1)}), bf16[32,44,384]{2,1,0:T(8,128)(2,1)}) %all-gather.15.cloned.1.call-update) | async-done | bytes 1081360 | tf_op jit(solution)/shard_map/all_gather | solution.py:46
  225.1 2.2 reshape.123
  227.3 53.9 %all-gather.11.cloned.1.call-done = bf16[384,1408]{1,0:T(8,128)(2,1)} async-done(((bf16[24,1408]{1,0:T(8,128)(2,1)}), bf16[384,1408]{1,0:T(8,128)(2,1)}) %all-gather.11.cloned.1.call-update) | async-done | bytes 1081360 | tf_op jit(solution)/shard_map/all_gather | solution.py:22
  281.2 5.5 %convolution_convert_fusion = bf16[384,1408]{1,0:T(8,128)(2,1)} fusion(bf16[1408,384]{1,0:T(8,128)(2,1)} %reshape.123, bf16[384,1408]{1,0:T(8,128)(2,1)} %all-gather.11.cloned.1.call-done, bf16[1408,384]{1,0:T(8,128)(2,1)} %reshape.121), kind=kOutput, calls=%fused_computation | convolution fusion | flops 840597504 | bytes 4325376 | tf_op jit(solution)/shard_map/dot_general | solution.py:30
  286.7 0.0 reduce-scatter.9.cloned.1.call-update
  286.8 0.0 all-gather.17.cloned.1.call-start
  286.8 0.6 copy-done.5
  287.4 87.0 %reduce-scatter.9.cloned.1.call-done = bf16[24,1408]{1,0:T(8,128)(2,1)} async-done(((bf16[384,1408]{1,0:T(8,128)(2,1)}), bf16[24,1408]{1,0:T(8,128)(2,1)}) %reduce-scatter.9.cloned.1.call-update) | async-done | bytes 67600
  374.4 1.0 convert_reduce_fusion.2
  375.5 1.1 fusion.61
  376.6 1.0 fusion.63
  377.5 0.7 reshape.124
  378.2 0.0 all-gather.17.cloned.1.call-update
  378.3 0.1 reshape.113
  378.4 0.1 subtract_reduce_fusion
  378.5 0.2 convert_reduce_fusion.3
  378.7 0.1 select_reduce_fusion
  378.8 57.7 %all-gather.17.cloned.1.call-done = bf16[16,6,5632]{2,1,0:T(8,128)(2,1)} async-done(((bf16[1,6,5632]{2,1,0:T(8,128)(2,1)}), bf16[16,6,5632]{2,1,0:T(8,128)(2,1)}) %all-gather.17.cloned.1.call-update) | async-done | bytes 1081360 | tf_op jit(solution)/shard_map/all_gather | solution.py:22
  436.5 2.3 reshape.125
  438.8 2.1 convolution_convert_fusion.2
  441.0 36.8 %all_to_all.5 = bf16[32,16,256]{2,1,0:T(8,128)(2,1)S(1)} all-to-all(bf16[32,16,256]{2,1,0:T(8,128)(2,1)S(1)} %bitcast.51), channel_id=1, replica_groups=mesh['tok'=32,'feat'=16] {'tok'}, dimensions={0} | all-to-all | bytes 524288 | tf_op jit(solution)/shard_map/all_to_all | solution.py:86
  477.8 0.7 copy.13
  (22 shorter events, 0.1 us)
Async XLA Ops:
  7.4 431.5 %copy-start = (bf16[5632,256]{1,0:T(8,128)(2,1)S(1)}, bf16[5632,256]{1,0:T(8,128)(2,1)}, u32[]{:S(2)}) copy-start(bf16[5632,256]{1,0:T(8,128)(2,1)} %param.18) | copy-start | bytes 8650756
  7.4 66.7 %all-gather.9.cloned.1.call-start = ((), (), s32[]{:S(2)}) async-start(), calls=%async_computation.3 | async-start | bytes 1148928 | tf_op jit(solution)/shard_map/all_gather | solution.py:22
  11.9 64.2 %copy-start.3 = (s32[384]{0:T(512)S(1)}, s32[384]{0:T(512)}, u32[]{:S(2)}) copy-start(s32[384]{0:T(512)} %param.12) | copy-start | bytes 4612
  12.0 155.0 %reduce-scatter.7.cloned.1.call-start = ((), (), s32[]{:S(2)}) async-start(), calls=%async_computation.8 | async-start | bytes 1148928
  76.1 0.7 copy-start.2
  79.6 1.2 copy-start.4
  79.6 87.4 %copy-start.1 = (bf16[24,1408]{1,0:T(8,128)(2,1)S(1)}, bf16[24,1408]{1,0:T(8,128)(2,1)}, u32[]{:S(2)}) copy-start(bf16[24,1408]{1,0:T(8,128)(2,1)} %param.11) | copy-start | bytes 202756
  79.6 89.4 %all-gather.13.cloned.1.call-start = ((), (), s32[]{:S(2)}) async-start(), calls=%async_computation.5 | async-start | bytes 1216512 | tf_op jit(solution)/shard_map/all_gather | solution.py:42
  80.2 144.9 %all-gather.15.cloned.1.call-start = ((), (), s32[]{:S(2)}) async-start(), calls=%async_computation.6 | async-start | bytes 1216512 | tf_op jit(solution)/shard_map/all_gather | solution.py:46
  80.8 200.4 %all-gather.11.cloned.1.call-start = ((), (), s32[]{:S(2)}) async-start(), calls=%async_computation.4 | async-start | bytes 1148928 | tf_op jit(solution)/shard_map/all_gather | solution.py:22
  169.0 205.5 %reduce-scatter.9.cloned.1.call-start = ((), (), s32[]{:S(2)}) async-start(), calls=%async_computation.9 | async-start | bytes 1148928
  286.7 0.7 copy-start.5
  286.7 91.9 %copy-start.6 = (s32[32]{0:T(128)S(1)}, s32[32]{0:T(128)}, u32[]{:S(2)}) copy-start(s32[32]{0:T(128)} %param.13) | copy-start | bytes 388
  286.8 149.8 %all-gather.17.cloned.1.call-start = ((), (), s32[]{:S(2)}) async-start(), calls=%async_computation.7 | async-start | bytes 1531904 | tf_op jit(solution)/shard_map/all_gather | solution.py:22
Sparse Core Ops, SparseCore 0:
  12.1 61.9 all-gather.8
  79.7 87.1 reduce-scatter.6
  286.9 87.5 reduce-scatter.8
Sparse Core Ops, SparseCore 1:
  82.2 72.5 all-gather.12
  156.7 68.3 all-gather.14
  228.0 53.2 all-gather.10
  378.3 58.1 all-gather.16
where the time goes:
time: 486 us
  waiting for transfers between devices  402 us (83%)
  blocking collectives  36.8 us (8%)
  between operations  14.9 us (3%)
  matrix products  12.6 us (3%)
  other arithmetic  10.1 us (2%)
  local copies, waits for them, and re-layouts  9.2 us (2%)
    unnamed x9, waiting for transfers between devices  174 us
    all_gather x3, waiting for transfers between devices, project_rows(): lax.all_gather(row_block, 'feat', axis=0, tiled=True)  174 us
    all_gather x1, waiting for transfers between devices, lower_weight(): return lax.all_gather(fetched[1], 'tok', axis=1, tiled=True)  53.8 us
    all_to_all x1, blocking collectives, route_rows(): lax.all_to_all(packed, 'tok', split_axis=0, concat_axis=0, tiled=True)  36.8 us
  transfers between devices with their start and end apart: 7, of which 6 were waited for; matrix products, arithmetic and copies ran while one was open for 1% of the time, Pallas kernels for 0%

commit v1 on v0

--- a/solution.py
+++ b/solution.py
@@ -1,3 +1,4 @@
+import functools
 import jax
 import jax.numpy as jnp
 from jax import lax
@@ -7,6 +8,23 @@
 MOST_UNITS = 16
 HEAD_DIM = 88
 epsilon = 1e-06
+
+
+def write_corner(buf, mesh_name):
+    extent = lax.axis_size(mesh_name)
+    row_list = [(at, (at + 1) % extent) for at in range(extent)]
+    kept_rows = [(at, (at - 1) % extent) for at in range(extent)]
+    low, base_arr = ([buf], [buf])
+    for _ in range(extent // 2):
+        low.append(lax.ppermute(low[-1], mesh_name, row_list))
+    for _ in tuple(range((extent - 1) // 2)):
+        base_arr.append(lax.ppermute(base_arr[-1], mesh_name, kept_rows))
+    a_next = jnp.concatenate([*low[::-1], *base_arr[1:]], 0)
+    arr_next = jnp.roll(a_next, (lax.axis_index(mesh_name) - extent // 2) * buf.shape[0], axis=0)
+    return arr_next
+
+
+drive_bands_over_axis = functools.partial(write_corner, mesh_name="feat")
 
 
 def layer_norm(row_block, gain_row):
@@ -19,9 +37,7 @@
 
 def project_rows(row_block, weight_block):
     return jnp.dot(
-        lax.all_gather(row_block, "feat", axis=0, tiled=True),
-        weight_block,
-        preferred_element_type=jnp.float32,
+        drive_bands_over_axis(row_block), weight_block, preferred_element_type=jnp.float32
     )
 
 

time: 486 us -> 579 us (1.19)
  waiting for transfers between devices: 402 us -> 203 us
  starting transfers between devices: 0.25 us -> 190 us
  local copies, waits for them, and re-layouts: 9.2 us -> 97.9 us
  blocking collectives: 36.8 us -> 43.9 us
    ppermute x0 -> x45, starting transfers between devices: none -> 190 us  [the longest x21 140 us: write_corner(): base_arr.append(lax.ppermute(base_arr[-1], mesh_name, kept_rows))]
    all_gather x3 -> x0, waiting for transfers between devices: 174 us -> none  [project_rows(): lax.all_gather(row_block, 'feat', axis=0, tiled=True)]
    concatenate x0 -> x3, local copies, waits for them, and re-layouts: none -> 70.9 us  [the longest x1 70.2 us: write_corner(): jnp.roll(a_next, (lax.axis_index(mesh_name) - extent // 2) * buf.shape[0]...]
    all_gather x1, waiting for transfers between devices: 53.8 us -> 0.01 us  [lower_weight(): return lax.all_gather(fetched[1], 'tok', axis=1, tiled=True)]
    ppermute x0 -> x45, waiting for transfers between devices: none -> 18.3 us  [the longest x24 18.3 us: write_corner(): low.append(lax.ppermute(low[-1], mesh_name, row_list))]
    unnamed x19 -> x63, local copies, waits for them, and re-layouts: 9.1 us -> 26.3 us
    unnamed x9 -> x6, waiting for transfers between devices: 174 us -> 185 us
    all_to_all x1, blocking collectives: 36.8 us -> 43.9 us  [route_rows(): lax.all_to_all(packed, 'tok', split_axis=0, concat_axis=0, tiled=True)]
  transfers between devices with their start and end apart: 7 -> 49, of which waited for: 6 -> 6; matrix products, arithmetic and copies ran while one was open for 1% -> 5% of each run, Pallas kernels for 0% -> 0%
where the time goes in v1:
time: 579 us; the launch traced here: 573 us
  waiting for transfers between devices  203 us (35%)
  starting transfers between devices  190 us (33%)
  local copies, waits for them, and re-layouts  97.9 us (17%)
  blocking collectives  43.9 us (8%)
  between operations  15.9 us (3%)
  matrix products  12.1 us (2%)
  other arithmetic  10.4 us (2%)
    unnamed x6, waiting for transfers between devices  185 us
    ppermute x21, starting transfers between devices, write_corner(): base_arr.append(lax.ppermute(base_arr[-1], mesh_name, kept_rows))  140 us
    concatenate x1, local copies, waits for them, and re-layouts, write_corner(): jnp.roll(a_next, (lax.axis_index(mesh_name) - extent // 2) * buf.shape[0]...  70.2 us
    ppermute x24, starting transfers between devices, write_corner(): low.append(lax.ppermute(low[-1], mesh_name, row_list))  49.3 us
    all_to_all x1, blocking collectives, route_rows(): lax.all_to_all(packed, 'tok', split_axis=0, concat_axis=0, tiled=True)  43.9 us
    unnamed x63, local copies, waits for them, and re-layouts  26.3 us
    ppermute x24, waiting for transfers between devices, write_corner(): low.append(lax.ppermute(low[-1], mesh_name, row_list))  18.3 us
  transfers between devices with their start and end apart: 49, of which 6 were waited for; matrix products, arithmetic and copies ran while one was open for 5% of the time, Pallas kernels for 0%

profile of v1, /device:TPU:1, one launch (start us, length us, event | category | flops | bytes accessed | tf_op | source)
XLA Modules:
  0.0 573.1 jit_solution(12973640996930477600)
XLA Ops:
  11.3 3.9 collective-permute-start
  15.3 5.4 collective-permute-done
  22.6 6.7 %collective-permute-start.8 = (bf16[24,1408]{1,0:T(8,128)(2,1)S(1)}, bf16[24,1408]{1,0:T(8,128)(2,1)S(1)}, u32[]{:S(2)}, u32[]{:S(2)}) collective-permute-start(bf16[24,1408]{1,0:T(8,128)(2,1)S(1)} %fusion.70), channel_id=1, source_target_pairs={{0,15},{1,0},{2,1},{3,2},{4,3},{5,4},{6,5},{7,6},{8,7},{9,8},{10,9... | collective-permute-start | bytes 202760 | tf_op jit(solution)/shard_map/ppermute | solution.py:21
  29.3 1.9 collective-permute-start.2
  31.2 6.7 %collective-permute-start.9 = (bf16[24,1408]{1,0:T(8,128)(2,1)S(1)}, bf16[24,1408]{1,0:T(8,128)(2,1)S(1)}, u32[]{:S(2)}, u32[]{:S(2)}) collective-permute-start(bf16[24,1408]{1,0:T(8,128)(2,1)S(1)} %collective-permute-done.8), channel_id=1, source_target_pairs={{0,15},{1,0},{2,1},{3,2},{4,3},{5,4},{6,5},{7,6},{8,7},{9,8},{10,9... | collective-permute-start | bytes 202760 | tf_op jit(solution)/shard_map/ppermute | solution.py:21
  37.9 1.9 collective-permute-start.3
  39.8 6.7 %collective-permute-start.10 = (bf16[24,1408]{1,0:T(8,128)(2,1)S(1)}, bf16[24,1408]{1,0:T(8,128)(2,1)S(1)}, u32[]{:S(2)}, u32[]{:S(2)}) collective-permute-start(bf16[24,1408]{1,0:T(8,128)(2,1)S(1)} %collective-permute-done.9), channel_id=1, source_target_pairs={{0,15},{1,0},{2,1},{3,2},{4,3},{5,4},{6,5},{7,6},{8,7},{9,8},{10,9... | collective-permute-start | bytes 202760 | tf_op jit(solution)/shard_map/ppermute | solution.py:21
  48.6 7.2 %collective-permute-start.11 = (bf16[24,1408]{1,0:T(8,128)(2,1)S(1)}, bf16[24,1408]{1,0:T(8,128)(2,1)S(1)}, u32[]{:S(2)}, u32[]{:S(2)}) collective-permute-start(bf16[24,1408]{1,0:T(8,128)(2,1)S(1)} %collective-permute-done.10), channel_id=1, source_target_pairs={{0,15},{1,0},{2,1},{3,2},{4,3},{5,4},{6,5},{7,6},{8,7},{9,8},{10,9... | collective-permute-start | bytes 202760 | tf_op jit(solution)/shard_map/ppermute | solution.py:21
  55.9 1.9 collective-permute-start.5
  57.8 6.7 %collective-permute-start.12 = (bf16[24,1408]{1,0:T(8,128)(2,1)S(1)}, bf16[24,1408]{1,0:T(8,128)(2,1)}, u32[]{:S(2)}, u32[]{:S(2)}) collective-permute-start(bf16[24,1408]{1,0:T(8,128)(2,1)S(1)} %collective-permute-done.11), channel_id=1, source_target_pairs={{0,15},{1,0},{2,1},{3,2},{4,3},{5,4},{6,5},{7,6},{8,7},{9,8},{10,9... | collective-permute-start | bytes 202760 | tf_op jit(solution)/shard_map/ppermute | solution.py:21
  64.6 1.9 collective-permute-start.6
  66.5 6.7 %collective-permute-start.13 = (bf16[24,1408]{1,0:T(8,128)(2,1)}, bf16[24,1408]{1,0:T(8,128)(2,1)}, u32[]{:S(2)}, u32[]{:S(2)}) collective-permute-start(bf16[24,1408]{1,0:T(8,128)(2,1)} %collective-permute-done.12), channel_id=1, source_target_pairs={{0,15},{1,0},{2,1},{3,2},{4,3},{5,4},{6,5},{7,6},{8,7},{9,8},{10,9... | collective-permute-start | bytes 202760 | tf_op jit(solution)/shard_map/ppermute | solution.py:21
  73.2 1.9 collective-permute-start.7
  75.2 6.8 %collective-permute-start.14 = (bf16[24,1408]{1,0:T(8,128)(2,1)}, bf16[24,1408]{1,0:T(8,128)(2,1)S(1)}, u32[]{:S(2)}, u32[]{:S(2)}) collective-permute-start(bf16[24,1408]{1,0:T(8,128)(2,1)} %collective-permute-done.13), channel_id=1, source_target_pairs={{0,15},{1,0},{2,1},{3,2},{4,3},{5,4},{6,5},{7,6},{8,7},{9,8},{10,9... | collective-permute-start | bytes 202760 | tf_op jit(solution)/shard_map/ppermute | solution.py:21
  89.8 2.7 convolution_convert_fusion.1
  93.7 92.6 %reduce-scatter.7.cloned.1.call-done = bf16[24,1408]{1,0:T(8,128)(2,1)} async-done(((bf16[384,1408]{1,0:T(8,128)(2,1)}), bf16[24,1408]{1,0:T(8,128)(2,1)}) %reduce-scatter.7.cloned.1.call-update) | async-done | bytes 67600
  187.6 2.5 collective-permute-start.15
  190.1 5.9 %collective-permute-done.15 = bf16[24,1408]{1,0:T(8,128)(2,1)S(1)} collective-permute-done((bf16[24,1408]{1,0:T(8,128)(2,1)S(1)}, bf16[24,1408]{1,0:T(8,128)(2,1)S(1)}, u32[]{:S(2)}, u32[]{:S(2)}) %collective-permute-start.15) | collective-permute-done | bytes 67616 | tf_op jit(solution)/shard_map/ppermute | solution.py:19
  197.9 6.7 %collective-permute-start.23 = (bf16[24,1408]{1,0:T(8,128)(2,1)S(1)}, bf16[24,1408]{1,0:T(8,128)(2,1)S(1)}, u32[]{:S(2)}, u32[]{:S(2)}) collective-permute-start(bf16[24,1408]{1,0:T(8,128)(2,1)S(1)} %fusion.67), channel_id=1, source_target_pairs={{0,15},{1,0},{2,1},{3,2},{4,3},{5,4},{6,5},{7,6},{8,7},{9,8},{10,9... | collective-permute-start | bytes 202760 | tf_op jit(solution)/shard_map/ppermute | solution.py:21
  206.5 6.7 %collective-permute-start.24 = (bf16[24,1408]{1,0:T(8,128)(2,1)S(1)}, bf16[24,1408]{1,0:T(8,128)(2,1)S(1)}, u32[]{:S(2)}, u32[]{:S(2)}) collective-permute-start(bf16[24,1408]{1,0:T(8,128)(2,1)S(1)} %collective-permute-done.23), channel_id=1, source_target_pairs={{0,15},{1,0},{2,1},{3,2},{4,3},{5,4},{6,5},{7,6},{8,7},{9,8},{10,9... | collective-permute-start | bytes 202760 | tf_op jit(solution)/shard_map/ppermute | solution.py:21
  213.2 1.9 collective-permute-start.18
  215.2 6.7 %collective-permute-start.25 = (bf16[24,1408]{1,0:T(8,128)(2,1)S(1)}, bf16[24,1408]{1,0:T(8,128)(2,1)S(1)}, u32[]{:S(2)}, u32[]{:S(2)}) collective-permute-start(bf16[24,1408]{1,0:T(8,128)(2,1)S(1)} %collective-permute-done.24), channel_id=1, source_target_pairs={{0,15},{1,0},{2,1},{3,2},{4,3},{5,4},{6,5},{7,6},{8,7},{9,8},{10,9... | collective-permute-start | bytes 202760 | tf_op jit(solution)/shard_map/ppermute | solution.py:21
  223.8 6.7 %collective-permute-start.26 = (bf16[24,1408]{1,0:T(8,128)(2,1)S(1)}, bf16[24,1408]{1,0:T(8,128)(2,1)S(1)}, u32[]{:S(2)}, u32[]{:S(2)}) collective-permute-start(bf16[24,1408]{1,0:T(8,128)(2,1)S(1)} %collective-permute-done.25), channel_id=1, source_target_pairs={{0,15},{1,0},{2,1},{3,2},{4,3},{5,4},{6,5},{7,6},{8,7},{9,8},{10,9... | collective-permute-start | bytes 202760 | tf_op jit(solution)/shard_map/ppermute | solution.py:21
  232.4 6.7 %collective-permute-start.27 = (bf16[24,1408]{1,0:T(8,128)(2,1)S(1)}, bf16[24,1408]{1,0:T(8,128)(2,1)}, u32[]{:S(2)}, u32[]{:S(2)}) collective-permute-start(bf16[24,1408]{1,0:T(8,128)(2,1)S(1)} %collective-permute-done.26), channel_id=1, source_target_pairs={{0,15},{1,0},{2,1},{3,2},{4,3},{5,4},{6,5},{7,6},{8,7},{9,8},{10,9... | collective-permute-start | bytes 202760 | tf_op jit(solution)/shard_map/ppermute | solution.py:21
  239.2 1.9 collective-permute-start.21
  241.1 6.7 %collective-permute-start.28 = (bf16[24,1408]{1,0:T(8,128)(2,1)}, bf16[24,1408]{1,0:T(8,128)(2,1)}, u32[]{:S(2)}, u32[]{:S(2)}) collective-permute-start(bf16[24,1408]{1,0:T(8,128)(2,1)} %collective-permute-done.27), channel_id=1, source_target_pairs={{0,15},{1,0},{2,1},{3,2},{4,3},{5,4},{6,5},{7,6},{8,7},{9,8},{10,9... | collective-permute-start | bytes 202760 | tf_op jit(solution)/shard_map/ppermute | solution.py:21
  247.8 1.9 collective-permute-start.22
  249.8 2.2 reshape.121
  251.9 2.1 reshape.123
  254.1 6.7 %collective-permute-start.29 = (bf16[24,1408]{1,0:T(8,128)(2,1)}, bf16[24,1408]{1,0:T(8,128)(2,1)S(1)}, u32[]{:S(2)}, u32[]{:S(2)}) collective-permute-start(bf16[24,1408]{1,0:T(8,128)(2,1)} %collective-permute-done.28), channel_id=1, source_target_pairs={{0,15},{1,0},{2,1},{3,2},{4,3},{5,4},{6,5},{7,6},{8,7},{9,8},{10,9... | collective-permute-start | bytes 202760 | tf_op jit(solution)/shard_map/ppermute | solution.py:21
  276.3 5.7 %convolution_convert_fusion = bf16[384,1408]{1,0:T(8,128)(2,1)} fusion(bf16[1408,384]{1,0:T(8,128)(2,1)} %reshape.123, bf16[1408,384]{1,0:T(8,128)(2,1)} %reshape.121, s32[]{:T(128)S(6)} %select_n.36, bf16[384,1408]{1,0:T(8,128)(2,1)} %constant_dynamic-update-slice_fusion.16), kind=kOutput, calls=%fused_computation | convolution fusion | flops 842760192 | bytes 4325380 | tf_op jit(solution)/shard_map/dot_general | solution.py:46
  282.7 90.9 %reduce-scatter.9.cloned.1.call-done = bf16[24,1408]{1,0:T(8,128)(2,1)} async-done(((bf16[384,1408]{1,0:T(8,128)(2,1)}), bf16[24,1408]{1,0:T(8,128)(2,1)}) %reduce-scatter.9.cloned.1.call-update) | async-done | bytes 67600
  376.8 2.4 collective-permute-start.30
  379.2 6.2 %collective-permute-start.38 = (bf16[6,5632]{1,0:T(8,128)(2,1)S(1)}, bf16[6,5632]{1,0:T(8,128)(2,1)S(1)}, u32[]{:S(2)}, u32[]{:S(2)}) collective-permute-start(bf16[6,5632]{1,0:T(8,128)(2,1)S(1)} %reshape.117), channel_id=1, source_target_pairs={{0,15},{1,0},{2,1},{3,2},{4,3},{5,4},{6,5},{7,6},{8,7},{9,8},{10,9... | collective-permute-start | bytes 202760 | tf_op jit(solution)/shard_map/ppermute | solution.py:21
  385.4 1.9 collective-permute-start.31
  387.3 6.7 %collective-permute-start.39 = (bf16[6,5632]{1,0:T(8,128)(2,1)S(1)}, bf16[6,5632]{1,0:T(8,128)(2,1)S(1)}, u32[]{:S(2)}, u32[]{:S(2)}) collective-permute-start(bf16[6,5632]{1,0:T(8,128)(2,1)S(1)} %collective-permute-done.38), channel_id=1, source_target_pairs={{0,15},{1,0},{2,1},{3,2},{4,3},{5,4},{6,5},{7,6},{8,7},{9,8},{10,9... | collective-permute-start | bytes 202760 | tf_op jit(solution)/shard_map/ppermute | solution.py:21
  396.0 6.7 %collective-permute-start.40 = (bf16[6,5632]{1,0:T(8,128)(2,1)S(1)}, bf16[6,5632]{1,0:T(8,128)(2,1)S(1)}, u32[]{:S(2)}, u32[]{:S(2)}) collective-permute-start(bf16[6,5632]{1,0:T(8,128)(2,1)S(1)} %collective-permute-done.39), channel_id=1, source_target_pairs={{0,15},{1,0},{2,1},{3,2},{4,3},{5,4},{6,5},{7,6},{8,7},{9,8},{10,9... | collective-permute-start | bytes 202760 | tf_op jit(solution)/shard_map/ppermute | solution.py:21
  402.7 1.9 collective-permute-start.33
  405.3 6.7 %collective-permute-start.41 = (bf16[6,5632]{1,0:T(8,128)(2,1)S(1)}, bf16[6,5632]{1,0:T(8,128)(2,1)S(1)}, u32[]{:S(2)}, u32[]{:S(2)}) collective-permute-start(bf16[6,5632]{1,0:T(8,128)(2,1)S(1)} %collective-permute-done.40), channel_id=1, source_target_pairs={{0,15},{1,0},{2,1},{3,2},{4,3},{5,4},{6,5},{7,6},{8,7},{9,8},{10,9... | collective-permute-start | bytes 202760 | tf_op jit(solution)/shard_map/ppermute | solution.py:21
  415.5 6.7 %collective-permute-start.42 = (bf16[6,5632]{1,0:T(8,128)(2,1)S(1)}, bf16[6,5632]{1,0:T(8,128)(2,1)S(1)}, u32[]{:S(2)}, u32[]{:S(2)}) collective-permute-start(bf16[6,5632]{1,0:T(8,128)(2,1)S(1)} %collective-permute-done.41), channel_id=1, source_target_pairs={{0,15},{1,0},{2,1},{3,2},{4,3},{5,4},{6,5},{7,6},{8,7},{9,8},{10,9... | collective-permute-start | bytes 202760 | tf_op jit(solution)/shard_map/ppermute | solution.py:21
  424.3 6.7 %collective-permute-start.43 = (bf16[6,5632]{1,0:T(8,128)(2,1)S(1)}, bf16[6,5632]{1,0:T(8,128)(2,1)}, u32[]{:S(2)}, u32[]{:S(2)}) collective-permute-start(bf16[6,5632]{1,0:T(8,128)(2,1)S(1)} %collective-permute-done.42), channel_id=1, source_target_pairs={{0,15},{1,0},{2,1},{3,2},{4,3},{5,4},{6,5},{7,6},{8,7},{9,8},{10,9... | collective-permute-start | bytes 202760 | tf_op jit(solution)/shard_map/ppermute | solution.py:21
  431.1 1.9 collective-permute-start.36
  433.1 6.7 %collective-permute-start.44 = (bf16[6,5632]{1,0:T(8,128)(2,1)}, bf16[6,5632]{1,0:T(8,128)(2,1)}, u32[]{:S(2)}, u32[]{:S(2)}) collective-permute-start(bf16[6,5632]{1,0:T(8,128)(2,1)} %collective-permute-done.43), channel_id=1, source_target_pairs={{0,15},{1,0},{2,1},{3,2},{4,3},{5,4},{6,5},{7,6},{8,7},{9,8},{10,9... | collective-permute-start | bytes 202760 | tf_op jit(solution)/shard_map/ppermute | solution.py:21
  439.8 2.1 collective-permute-start.37
  442.0 6.8 %collective-permute-done.37 = bf16[6,5632]{1,0:T(8,128)(2,1)} collective-permute-done((bf16[6,5632]{1,0:T(8,128)(2,1)}, bf16[6,5632]{1,0:T(8,128)(2,1)}, u32[]{:S(2)}, u32[]{:S(2)}) %collective-permute-start.37) | collective-permute-done | bytes 67616 | tf_op jit(solution)/shard_map/ppermute | solution.py:19
  448.8 70.2 %concatenate.17 = bf16[192,5632]{1,0:T(8,128)(2,1)} concatenate(bf16[6,5632]{1,0:T(8,128)(2,1)} %collective-permute-done.37, bf16[6,5632]{1,0:T(8,128)(2,1)} %collective-permute-done.36, bf16[6,5632]{1,0:T(8,128)(2,1)} %copy-done.5, bf16[6,5632]{1,0:T(8,128)(2,1)} %copy-done.3, bf16[6,5632]{1,0:T(8,128)(2,1)} %collective-permute-done.33, ...), dimensions={0} | concatenate | bytes 4325376 | tf_op jit(solution)/shard_map/jit(_roll_dynamic)/concatenate | solution.py:23
  519.0 2.1 convolution_convert_fusion.2
  521.1 43.9 %all_to_all.5 = bf16[32,16,256]{2,1,0:T(8,128)(2,1)S(1)} all-to-all(bf16[32,16,256]{2,1,0:T(8,128)(2,1)S(1)} %bitcast.49), channel_id=1, replica_groups=mesh['tok'=32,'feat'=16] {'tok'}, dimensions={0} | all-to-all | bytes 524288 | tf_op jit(solution)/shard_map/all_to_all | solution.py:102
  (153 shorter events, 54.2 us)
Async XLA Ops:
  7.4 178.9 %reduce-scatter.7.cloned.1.call-start = ((), (), s32[]{:S(2)}) async-start(), calls=%async_computation.5 | async-start | bytes 1148928
  11.3 9.3 %collective-permute-start = (bf16[24,1408]{1,0:T(8,128)(2,1)S(1)}, bf16[24,1408]{1,0:T(8,128)(2,1)S(1)}, u32[]{:S(2)}, u32[]{:S(2)}) collective-permute-start(bf16[24,1408]{1,0:T(8,128)(2,1)S(1)} %fusion.70), channel_id=1, source_target_pairs={{0,1},{1,2},{2,3},{3,4},{4,5},{5,6},{6,7},{7,8},{8,9},{9,10},{10,1... | collective-permute-start | bytes 202760 | tf_op jit(solution)/shard_map/ppermute | solution.py:19
  20.6 8.6 %collective-permute-start.1 = (bf16[24,1408]{1,0:T(8,128)(2,1)S(1)}, bf16[24,1408]{1,0:T(8,128)(2,1)S(1)}, u32[]{:S(2)}, u32[]{:S(2)}) collective-permute-start(bf16[24,1408]{1,0:T(8,128)(2,1)S(1)} %collective-permute-done), channel_id=1, source_target_pairs={{0,1},{1,2},{2,3},{3,4},{4,5},{5,6},{6,7},{7,8},{8,9},{9,10},{10,1... | collective-permute-start | bytes 202760 | tf_op jit(solution)/shard_map/ppermute | solution.py:19
  22.6 8.6 %collective-permute-start.8 = (bf16[24,1408]{1,0:T(8,128)(2,1)S(1)}, bf16[24,1408]{1,0:T(8,128)(2,1)S(1)}, u32[]{:S(2)}, u32[]{:S(2)}) collective-permute-start(bf16[24,1408]{1,0:T(8,128)(2,1)S(1)} %fusion.70), channel_id=1, source_target_pairs={{0,15},{1,0},{2,1},{3,2},{4,3},{5,4},{6,5},{7,6},{8,7},{9,8},{10,9... | collective-permute-start | bytes 202760 | tf_op jit(solution)/shard_map/ppermute | solution.py:21
  29.3 8.6 %collective-permute-start.2 = (bf16[24,1408]{1,0:T(8,128)(2,1)S(1)}, bf16[24,1408]{1,0:T(8,128)(2,1)S(1)}, u32[]{:S(2)}, u32[]{:S(2)}) collective-permute-start(bf16[24,1408]{1,0:T(8,128)(2,1)S(1)} %collective-permute-done.1), channel_id=1, source_target_pairs={{0,1},{1,2},{2,3},{3,4},{4,5},{5,6},{6,7},{7,8},{8,9},{9,10},{10,1... | collective-permute-start | bytes 202760 | tf_op jit(solution)/shard_map/ppermute | solution.py:19
  31.2 8.6 %collective-permute-start.9 = (bf16[24,1408]{1,0:T(8,128)(2,1)S(1)}, bf16[24,1408]{1,0:T(8,128)(2,1)S(1)}, u32[]{:S(2)}, u32[]{:S(2)}) collective-permute-start(bf16[24,1408]{1,0:T(8,128)(2,1)S(1)} %collective-permute-done.8), channel_id=1, source_target_pairs={{0,15},{1,0},{2,1},{3,2},{4,3},{5,4},{6,5},{7,6},{8,7},{9,8},{10,9... | collective-permute-start | bytes 202760 | tf_op jit(solution)/shard_map/ppermute | solution.py:21
  37.9 8.8 %collective-permute-start.3 = (bf16[24,1408]{1,0:T(8,128)(2,1)S(1)}, bf16[24,1408]{1,0:T(8,128)(2,1)S(1)}, u32[]{:S(2)}, u32[]{:S(2)}) collective-permute-start(bf16[24,1408]{1,0:T(8,128)(2,1)S(1)} %collective-permute-done.2), channel_id=1, source_target_pairs={{0,1},{1,2},{2,3},{3,4},{4,5},{5,6},{6,7},{7,8},{8,9},{9,10},{10,1... | collective-permute-start | bytes 202760 | tf_op jit(solution)/shard_map/ppermute | solution.py:19
  39.8 8.8 %collective-permute-start.10 = (bf16[24,1408]{1,0:T(8,128)(2,1)S(1)}, bf16[24,1408]{1,0:T(8,128)(2,1)S(1)}, u32[]{:S(2)}, u32[]{:S(2)}) collective-permute-start(bf16[24,1408]{1,0:T(8,128)(2,1)S(1)} %collective-permute-done.9), channel_id=1, source_target_pairs={{0,15},{1,0},{2,1},{3,2},{4,3},{5,4},{6,5},{7,6},{8,7},{9,8},{10,9... | collective-permute-start | bytes 202760 | tf_op jit(solution)/shard_map/ppermute | solution.py:21
  46.7 9.2 %collective-permute-start.4 = (bf16[24,1408]{1,0:T(8,128)(2,1)S(1)}, bf16[24,1408]{1,0:T(8,128)(2,1)S(1)}, u32[]{:S(2)}, u32[]{:S(2)}) collective-permute-start(bf16[24,1408]{1,0:T(8,128)(2,1)S(1)} %collective-permute-done.3), channel_id=1, source_target_pairs={{0,1},{1,2},{2,3},{3,4},{4,5},{5,6},{6,7},{7,8},{8,9},{9,10},{10,1... | collective-permute-start | bytes 202760 | tf_op jit(solution)/shard_map/ppermute | solution.py:19
  48.6 9.2 %collective-permute-start.11 = (bf16[24,1408]{1,0:T(8,128)(2,1)S(1)}, bf16[24,1408]{1,0:T(8,128)(2,1)S(1)}, u32[]{:S(2)}, u32[]{:S(2)}) collective-permute-start(bf16[24,1408]{1,0:T(8,128)(2,1)S(1)} %collective-permute-done.10), channel_id=1, source_target_pairs={{0,15},{1,0},{2,1},{3,2},{4,3},{5,4},{6,5},{7,6},{8,7},{9,8},{10,9... | collective-permute-start | bytes 202760 | tf_op jit(solution)/shard_map/ppermute | solution.py:21
  55.9 8.6 %collective-permute-start.5 = (bf16[24,1408]{1,0:T(8,128)(2,1)S(1)}, bf16[24,1408]{1,0:T(8,128)(2,1)S(1)}, u32[]{:S(2)}, u32[]{:S(2)}) collective-permute-start(bf16[24,1408]{1,0:T(8,128)(2,1)S(1)} %collective-permute-done.4), channel_id=1, source_target_pairs={{0,1},{1,2},{2,3},{3,4},{4,5},{5,6},{6,7},{7,8},{8,9},{9,10},{10,1... | collective-permute-start | bytes 202760 | tf_op jit(solution)/shard_map/ppermute | solution.py:19
  57.8 8.6 %collective-permute-start.12 = (bf16[24,1408]{1,0:T(8,128)(2,1)S(1)}, bf16[24,1408]{1,0:T(8,128)(2,1)}, u32[]{:S(2)}, u32[]{:S(2)}) collective-permute-start(bf16[24,1408]{1,0:T(8,128)(2,1)S(1)} %collective-permute-done.11), channel_id=1, source_target_pairs={{0,15},{1,0},{2,1},{3,2},{4,3},{5,4},{6,5},{7,6},{8,7},{9,8},{10,9... | collective-permute-start | bytes 202760 | tf_op jit(solution)/shard_map/ppermute | solution.py:21
  64.6 8.7 %collective-permute-start.6 = (bf16[24,1408]{1,0:T(8,128)(2,1)S(1)}, bf16[24,1408]{1,0:T(8,128)(2,1)}, u32[]{:S(2)}, u32[]{:S(2)}) collective-permute-start(bf16[24,1408]{1,0:T(8,128)(2,1)S(1)} %collective-permute-done.5), channel_id=1, source_target_pairs={{0,1},{1,2},{2,3},{3,4},{4,5},{5,6},{6,7},{7,8},{8,9},{9,10},{10,1... | collective-permute-start | bytes 202760 | tf_op jit(solution)/shard_map/ppermute | solution.py:19
  66.5 8.7 %collective-permute-start.13 = (bf16[24,1408]{1,0:T(8,128)(2,1)}, bf16[24,1408]{1,0:T(8,128)(2,1)}, u32[]{:S(2)}, u32[]{:S(2)}) collective-permute-start(bf16[24,1408]{1,0:T(8,128)(2,1)} %collective-permute-done.12), channel_id=1, source_target_pairs={{0,15},{1,0},{2,1},{3,2},{4,3},{5,4},{6,5},{7,6},{8,7},{9,8},{10,9... | collective-permute-start | bytes 202760 | tf_op jit(solution)/shard_map/ppermute | solution.py:21
  73.2 8.8 %collective-permute-start.7 = (bf16[24,1408]{1,0:T(8,128)(2,1)}, bf16[24,1408]{1,0:T(8,128)(2,1)}, u32[]{:S(2)}, u32[]{:S(2)}) collective-permute-start(bf16[24,1408]{1,0:T(8,128)(2,1)} %collective-permute-done.6), channel_id=1, source_target_pairs={{0,1},{1,2},{2,3},{3,4},{4,5},{5,6},{6,7},{7,8},{8,9},{9,10},{10,1... | collective-permute-start | bytes 202760 | tf_op jit(solution)/shard_map/ppermute | solution.py:19
  75.2 12.4 %collective-permute-start.14 = (bf16[24,1408]{1,0:T(8,128)(2,1)}, bf16[24,1408]{1,0:T(8,128)(2,1)S(1)}, u32[]{:S(2)}, u32[]{:S(2)}) collective-permute-start(bf16[24,1408]{1,0:T(8,128)(2,1)} %collective-permute-done.13), channel_id=1, source_target_pairs={{0,15},{1,0},{2,1},{3,2},{4,3},{5,4},{6,5},{7,6},{8,7},{9,8},{10,9... | collective-permute-start | bytes 202760 | tf_op jit(solution)/shard_map/ppermute | solution.py:21
  92.5 157.3 %all-gather.5.cloned.1.call-start = ((), (), s32[]{:S(2)}) async-start(), calls=%async_computation.3 | async-start | bytes 1216512 | tf_op jit(solution)/shard_map/all_gather | solution.py:58
  93.0 158.9 %all-gather.7.cloned.1.call-start = ((), (), s32[]{:S(2)}) async-start(), calls=%async_computation.4 | async-start | bytes 1216512 | tf_op jit(solution)/shard_map/all_gather | solution.py:62
  93.6 280.0 %reduce-scatter.9.cloned.1.call-start = ((), (), s32[]{:S(2)}) async-start(), calls=%async_computation.6 | async-start | bytes 1148928
  187.6 8.4 %collective-permute-start.15 = (bf16[24,1408]{1,0:T(8,128)(2,1)S(1)}, bf16[24,1408]{1,0:T(8,128)(2,1)S(1)}, u32[]{:S(2)}, u32[]{:S(2)}) collective-permute-start(bf16[24,1408]{1,0:T(8,128)(2,1)S(1)} %fusion.67), channel_id=1, source_target_pairs={{0,1},{1,2},{2,3},{3,4},{4,5},{5,6},{6,7},{7,8},{8,9},{9,10},{10,1... | collective-permute-start | bytes 202760 | tf_op jit(solution)/shard_map/ppermute | solution.py:19
  196.0 8.6 %collective-permute-start.16 = (bf16[24,1408]{1,0:T(8,128)(2,1)S(1)}, bf16[24,1408]{1,0:T(8,128)(2,1)S(1)}, u32[]{:S(2)}, u32[]{:S(2)}) collective-permute-start(bf16[24,1408]{1,0:T(8,128)(2,1)S(1)} %collective-permute-done.15), channel_id=1, source_target_pairs={{0,1},{1,2},{2,3},{3,4},{4,5},{5,6},{6,7},{7,8},{8,9},{9,10},{10,1... | collective-permute-start | bytes 202760 | tf_op jit(solution)/shard_map/ppermute | solution.py:19
  197.9 8.6 %collective-permute-start.23 = (bf16[24,1408]{1,0:T(8,128)(2,1)S(1)}, bf16[24,1408]{1,0:T(8,128)(2,1)S(1)}, u32[]{:S(2)}, u32[]{:S(2)}) collective-permute-start(bf16[24,1408]{1,0:T(8,128)(2,1)S(1)} %fusion.67), channel_id=1, source_target_pairs={{0,15},{1,0},{2,1},{3,2},{4,3},{5,4},{6,5},{7,6},{8,7},{9,8},{10,9... | collective-permute-start | bytes 202760 | tf_op jit(solution)/shard_map/ppermute | solution.py:21
  204.6 8.6 %collective-permute-start.17 = (bf16[24,1408]{1,0:T(8,128)(2,1)S(1)}, bf16[24,1408]{1,0:T(8,128)(2,1)S(1)}, u32[]{:S(2)}, u32[]{:S(2)}) collective-permute-start(bf16[24,1408]{1,0:T(8,128)(2,1)S(1)} %collective-permute-done.16), channel_id=1, source_target_pairs={{0,1},{1,2},{2,3},{3,4},{4,5},{5,6},{6,7},{7,8},{8,9},{9,10},{10,1... | collective-permute-start | bytes 202760 | tf_op jit(solution)/shard_map/ppermute | solution.py:19
  206.5 8.6 %collective-permute-start.24 = (bf16[24,1408]{1,0:T(8,128)(2,1)S(1)}, bf16[24,1408]{1,0:T(8,128)(2,1)S(1)}, u32[]{:S(2)}, u32[]{:S(2)}) collective-permute-start(bf16[24,1408]{1,0:T(8,128)(2,1)S(1)} %collective-permute-done.23), channel_id=1, source_target_pairs={{0,15},{1,0},{2,1},{3,2},{4,3},{5,4},{6,5},{7,6},{8,7},{9,8},{10,9... | collective-permute-start | bytes 202760 | tf_op jit(solution)/shard_map/ppermute | solution.py:21
  213.2 8.6 %collective-permute-start.18 = (bf16[24,1408]{1,0:T(8,128)(2,1)S(1)}, bf16[24,1408]{1,0:T(8,128)(2,1)S(1)}, u32[]{:S(2)}, u32[]{:S(2)}) collective-permute-start(bf16[24,1408]{1,0:T(8,128)(2,1)S(1)} %collective-permute-done.17), channel_id=1, source_target_pairs={{0,1},{1,2},{2,3},{3,4},{4,5},{5,6},{6,7},{7,8},{8,9},{9,10},{10,1... | collective-permute-start | bytes 202760 | tf_op jit(solution)/shard_map/ppermute | solution.py:19
  215.2 8.6 %collective-permute-start.25 = (bf16[24,1408]{1,0:T(8,128)(2,1)S(1)}, bf16[24,1408]{1,0:T(8,128)(2,1)S(1)}, u32[]{:S(2)}, u32[]{:S(2)}) collective-permute-start(bf16[24,1408]{1,0:T(8,128)(2,1)S(1)} %collective-permute-done.24), channel_id=1, source_target_pairs={{0,15},{1,0},{2,1},{3,2},{4,3},{5,4},{6,5},{7,6},{8,7},{9,8},{10,9... | collective-permute-start | bytes 202760 | tf_op jit(solution)/shard_map/ppermute | solution.py:21
  221.9 8.6 %collective-permute-start.19 = (bf16[24,1408]{1,0:T(8,128)(2,1)S(1)}, bf16[24,1408]{1,0:T(8,128)(2,1)S(1)}, u32[]{:S(2)}, u32[]{:S(2)}) collective-permute-start(bf16[24,1408]{1,0:T(8,128)(2,1)S(1)} %collective-permute-done.18), channel_id=1, source_target_pairs={{0,1},{1,2},{2,3},{3,4},{4,5},{5,6},{6,7},{7,8},{8,9},{9,10},{10,1... | collective-permute-start | bytes 202760 | tf_op jit(solution)/shard_map/ppermute | solution.py:19
  223.8 8.6 %collective-permute-start.26 = (bf16[24,1408]{1,0:T(8,128)(2,1)S(1)}, bf16[24,1408]{1,0:T(8,128)(2,1)S(1)}, u32[]{:S(2)}, u32[]{:S(2)}) collective-permute-start(bf16[24,1408]{1,0:T(8,128)(2,1)S(1)} %collective-permute-done.25), channel_id=1, source_target_pairs={{0,15},{1,0},{2,1},{3,2},{4,3},{5,4},{6,5},{7,6},{8,7},{9,8},{10,9... | collective-permute-start | bytes 202760 | tf_op jit(solution)/shard_map/ppermute | solution.py:21
  230.5 8.6 %collective-permute-start.20 = (bf16[24,1408]{1,0:T(8,128)(2,1)S(1)}, bf16[24,1408]{1,0:T(8,128)(2,1)S(1)}, u32[]{:S(2)}, u32[]{:S(2)}) collective-permute-start(bf16[24,1408]{1,0:T(8,128)(2,1)S(1)} %collective-permute-done.19), channel_id=1, source_target_pairs={{0,1},{1,2},{2,3},{3,4},{4,5},{5,6},{6,7},{7,8},{8,9},{9,10},{10,1... | collective-permute-start | bytes 202760 | tf_op jit(solution)/shard_map/ppermute | solution.py:19
  232.4 8.6 %collective-permute-start.27 = (bf16[24,1408]{1,0:T(8,128)(2,1)S(1)}, bf16[24,1408]{1,0:T(8,128)(2,1)}, u32[]{:S(2)}, u32[]{:S(2)}) collective-permute-start(bf16[24,1408]{1,0:T(8,128)(2,1)S(1)} %collective-permute-done.26), channel_id=1, source_target_pairs={{0,15},{1,0},{2,1},{3,2},{4,3},{5,4},{6,5},{7,6},{8,7},{9,8},{10,9... | collective-permute-start | bytes 202760 | tf_op jit(solution)/shard_map/ppermute | solution.py:21
  239.2 8.7 %collective-permute-start.21 = (bf16[24,1408]{1,0:T(8,128)(2,1)S(1)}, bf16[24,1408]{1,0:T(8,128)(2,1)}, u32[]{:S(2)}, u32[]{:S(2)}) collective-permute-start(bf16[24,1408]{1,0:T(8,128)(2,1)S(1)} %collective-permute-done.20), channel_id=1, source_target_pairs={{0,1},{1,2},{2,3},{3,4},{4,5},{5,6},{6,7},{7,8},{8,9},{9,10},{10,1... | collective-permute-start | bytes 202760 | tf_op jit(solution)/shard_map/ppermute | solution.py:19
  241.1 13.0 %collective-permute-start.28 = (bf16[24,1408]{1,0:T(8,128)(2,1)}, bf16[24,1408]{1,0:T(8,128)(2,1)}, u32[]{:S(2)}, u32[]{:S(2)}) collective-permute-start(bf16[24,1408]{1,0:T(8,128)(2,1)} %collective-permute-done.27), channel_id=1, source_target_pairs={{0,15},{1,0},{2,1},{3,2},{4,3},{5,4},{6,5},{7,6},{8,7},{9,8},{10,9... | collective-permute-start | bytes 202760 | tf_op jit(solution)/shard_map/ppermute | solution.py:21
  247.8 13.0 %collective-permute-start.22 = (bf16[24,1408]{1,0:T(8,128)(2,1)}, bf16[24,1408]{1,0:T(8,128)(2,1)}, u32[]{:S(2)}, u32[]{:S(2)}) collective-permute-start(bf16[24,1408]{1,0:T(8,128)(2,1)} %collective-permute-done.21), channel_id=1, source_target_pairs={{0,1},{1,2},{2,3},{3,4},{4,5},{5,6},{6,7},{7,8},{8,9},{9,10},{10,1... | collective-permute-start | bytes 202760 | tf_op jit(solution)/shard_map/ppermute | solution.py:19
  254.1 21.5 %collective-permute-start.29 = (bf16[24,1408]{1,0:T(8,128)(2,1)}, bf16[24,1408]{1,0:T(8,128)(2,1)S(1)}, u32[]{:S(2)}, u32[]{:S(2)}) collective-permute-start(bf16[24,1408]{1,0:T(8,128)(2,1)} %collective-permute-done.28), channel_id=1, source_target_pairs={{0,15},{1,0},{2,1},{3,2},{4,3},{5,4},{6,5},{7,6},{8,7},{9,8},{10,9... | collective-permute-start | bytes 202760 | tf_op jit(solution)/shard_map/ppermute | solution.py:21
  376.8 8.6 %collective-permute-start.30 = (bf16[6,5632]{1,0:T(8,128)(2,1)S(1)}, bf16[6,5632]{1,0:T(8,128)(2,1)S(1)}, u32[]{:S(2)}, u32[]{:S(2)}) collective-permute-start(bf16[6,5632]{1,0:T(8,128)(2,1)S(1)} %reshape.117), channel_id=1, source_target_pairs={{0,1},{1,2},{2,3},{3,4},{4,5},{5,6},{6,7},{7,8},{8,9},{9,10},{10,1... | collective-permute-start | bytes 202760 | tf_op jit(solution)/shard_map/ppermute | solution.py:19
  385.4 8.6 %collective-permute-start.31 = (bf16[6,5632]{1,0:T(8,128)(2,1)S(1)}, bf16[6,5632]{1,0:T(8,128)(2,1)S(1)}, u32[]{:S(2)}, u32[]{:S(2)}) collective-permute-start(bf16[6,5632]{1,0:T(8,128)(2,1)S(1)} %collective-permute-done.30), channel_id=1, source_target_pairs={{0,1},{1,2},{2,3},{3,4},{4,5},{5,6},{6,7},{7,8},{8,9},{9,10},{10,1... | collective-permute-start | bytes 202760 | tf_op jit(solution)/shard_map/ppermute | solution.py:19
  387.3 8.6 %collective-permute-start.39 = (bf16[6,5632]{1,0:T(8,128)(2,1)S(1)}, bf16[6,5632]{1,0:T(8,128)(2,1)S(1)}, u32[]{:S(2)}, u32[]{:S(2)}) collective-permute-start(bf16[6,5632]{1,0:T(8,128)(2,1)S(1)} %collective-permute-done.38), channel_id=1, source_target_pairs={{0,15},{1,0},{2,1},{3,2},{4,3},{5,4},{6,5},{7,6},{8,7},{9,8},{10,9... | collective-permute-start | bytes 202760 | tf_op jit(solution)/shard_map/ppermute | solution.py:21
  394.0 8.6 %collective-permute-start.32 = (bf16[6,5632]{1,0:T(8,128)(2,1)S(1)}, bf16[6,5632]{1,0:T(8,128)(2,1)S(1)}, u32[]{:S(2)}, u32[]{:S(2)}) collective-permute-start(bf16[6,5632]{1,0:T(8,128)(2,1)S(1)} %collective-permute-done.31), channel_id=1, source_target_pairs={{0,1},{1,2},{2,3},{3,4},{4,5},{5,6},{6,7},{7,8},{8,9},{9,10},{10,1... | collective-permute-start | bytes 202760 | tf_op jit(solution)/shard_map/ppermute | solution.py:19
  396.0 9.4 %collective-permute-start.40 = (bf16[6,5632]{1,0:T(8,128)(2,1)S(1)}, bf16[6,5632]{1,0:T(8,128)(2,1)S(1)}, u32[]{:S(2)}, u32[]{:S(2)}) collective-permute-start(bf16[6,5632]{1,0:T(8,128)(2,1)S(1)} %collective-permute-done.39), channel_id=1, source_target_pairs={{0,15},{1,0},{2,1},{3,2},{4,3},{5,4},{6,5},{7,6},{8,7},{9,8},{10,9... | collective-permute-start | bytes 202760 | tf_op jit(solution)/shard_map/ppermute | solution.py:21
  402.7 9.3 %collective-permute-start.33 = (bf16[6,5632]{1,0:T(8,128)(2,1)S(1)}, bf16[6,5632]{1,0:T(8,128)(2,1)}, u32[]{:S(2)}, u32[]{:S(2)}) collective-permute-start(bf16[6,5632]{1,0:T(8,128)(2,1)S(1)} %collective-permute-done.32), channel_id=1, source_target_pairs={{0,1},{1,2},{2,3},{3,4},{4,5},{5,6},{6,7},{7,8},{8,9},{9,10},{10,1... | collective-permute-start | bytes 202760 | tf_op jit(solution)/shard_map/ppermute | solution.py:19
  405.3 9.5 %collective-permute-start.41 = (bf16[6,5632]{1,0:T(8,128)(2,1)S(1)}, bf16[6,5632]{1,0:T(8,128)(2,1)S(1)}, u32[]{:S(2)}, u32[]{:S(2)}) collective-permute-start(bf16[6,5632]{1,0:T(8,128)(2,1)S(1)} %collective-permute-done.40), channel_id=1, source_target_pairs={{0,15},{1,0},{2,1},{3,2},{4,3},{5,4},{6,5},{7,6},{8,7},{9,8},{10,9... | collective-permute-start | bytes 202760 | tf_op jit(solution)/shard_map/ppermute | solution.py:21
  412.0 10.2 %collective-permute-start.34 = (bf16[6,5632]{1,0:T(8,128)(2,1)}, bf16[6,5632]{1,0:T(8,128)(2,1)S(1)}, u32[]{:S(2)}, u32[]{:S(2)}) collective-permute-start(bf16[6,5632]{1,0:T(8,128)(2,1)} %collective-permute-done.33), channel_id=1, source_target_pairs={{0,1},{1,2},{2,3},{3,4},{4,5},{5,6},{6,7},{7,8},{8,9},{9,10},{10,1... | collective-permute-start | bytes 202760 | tf_op jit(solution)/shard_map/ppermute | solution.py:19
  415.5 8.8 %collective-permute-start.42 = (bf16[6,5632]{1,0:T(8,128)(2,1)S(1)}, bf16[6,5632]{1,0:T(8,128)(2,1)S(1)}, u32[]{:S(2)}, u32[]{:S(2)}) collective-permute-start(bf16[6,5632]{1,0:T(8,128)(2,1)S(1)} %collective-permute-done.41), channel_id=1, source_target_pairs={{0,15},{1,0},{2,1},{3,2},{4,3},{5,4},{6,5},{7,6},{8,7},{9,8},{10,9... | collective-permute-start | bytes 202760 | tf_op jit(solution)/shard_map/ppermute | solution.py:21
  422.2 8.8 %collective-permute-start.35 = (bf16[6,5632]{1,0:T(8,128)(2,1)S(1)}, bf16[6,5632]{1,0:T(8,128)(2,1)S(1)}, u32[]{:S(2)}, u32[]{:S(2)}) collective-permute-start(bf16[6,5632]{1,0:T(8,128)(2,1)S(1)} %collective-permute-done.34), channel_id=1, source_target_pairs={{0,1},{1,2},{2,3},{3,4},{4,5},{5,6},{6,7},{7,8},{8,9},{9,10},{10,1... | collective-permute-start | bytes 202760 | tf_op jit(solution)/shard_map/ppermute | solution.py:19
  424.3 8.8 %collective-permute-start.43 = (bf16[6,5632]{1,0:T(8,128)(2,1)S(1)}, bf16[6,5632]{1,0:T(8,128)(2,1)}, u32[]{:S(2)}, u32[]{:S(2)}) collective-permute-start(bf16[6,5632]{1,0:T(8,128)(2,1)S(1)} %collective-permute-done.42), channel_id=1, source_target_pairs={{0,15},{1,0},{2,1},{3,2},{4,3},{5,4},{6,5},{7,6},{8,7},{9,8},{10,9... | collective-permute-start | bytes 202760 | tf_op jit(solution)/shard_map/ppermute | solution.py:21
  431.1 8.7 %collective-permute-start.36 = (bf16[6,5632]{1,0:T(8,128)(2,1)S(1)}, bf16[6,5632]{1,0:T(8,128)(2,1)}, u32[]{:S(2)}, u32[]{:S(2)}) collective-permute-start(bf16[6,5632]{1,0:T(8,128)(2,1)S(1)} %collective-permute-done.35), channel_id=1, source_target_pairs={{0,1},{1,2},{2,3},{3,4},{4,5},{5,6},{6,7},{7,8},{8,9},{9,10},{10,1... | collective-permute-start | bytes 202760 | tf_op jit(solution)/shard_map/ppermute | solution.py:19
  433.1 8.8 %collective-permute-start.44 = (bf16[6,5632]{1,0:T(8,128)(2,1)}, bf16[6,5632]{1,0:T(8,128)(2,1)}, u32[]{:S(2)}, u32[]{:S(2)}) collective-permute-start(bf16[6,5632]{1,0:T(8,128)(2,1)} %collective-permute-done.43), channel_id=1, source_target_pairs={{0,15},{1,0},{2,1},{3,2},{4,3},{5,4},{6,5},{7,6},{8,7},{9,8},{10,9... | collective-permute-start | bytes 202760 | tf_op jit(solution)/shard_map/ppermute | solution.py:21
  439.8 8.9 %collective-permute-start.37 = (bf16[6,5632]{1,0:T(8,128)(2,1)}, bf16[6,5632]{1,0:T(8,128)(2,1)}, u32[]{:S(2)}, u32[]{:S(2)}) collective-permute-start(bf16[6,5632]{1,0:T(8,128)(2,1)} %collective-permute-done.36), channel_id=1, source_target_pairs={{0,1},{1,2},{2,3},{3,4},{4,5},{5,6},{6,7},{7,8},{8,9},{9,10},{10,1... | collective-permute-start | bytes 202760 | tf_op jit(solution)/shard_map/ppermute | solution.py:19
  (17 other events, 815.5 us)
Sparse Core Ops, SparseCore 0:
  92.6 93.6 reduce-scatter.6
  282.1 91.4 reduce-scatter.8
Sparse Core Ops, SparseCore 1:
  95.0 78.9 all-gather.4
  176.0 68.3 all-gather.6
